TPU v7x, 256 devices: a whole 4x4x8 slice. The times are simulated.
256 devices in a mesh: pipe: 4 (over y), seq: 16 (over z, core), dp: 4 (over x).
Axes of the slice: x: 4, y: 4, z: 8, core: 2. Of those that a mesh axis runs over, the one named last changes fastest.
Arguments:
- section_inputs: bfloat16 [4, 4, 16, 16, 8, 512], P('pipe', 'dp', 'seq'), may hold values from -6 to 6
- w_spatial: bfloat16 [4, 9, 512, 512], P('pipe'), may hold values from -0.09375 to 0.09375
- w_temporal: bfloat16 [4, 3, 512, 512], P('pipe'), may hold values from -0.15625 to 0.15625
- grad_output: bfloat16 [4, 16, 16, 8, 512], P('dp', 'seq'), may hold values from -6 to 6
- frame_start: int32 [4], P('dp'), may hold values from 0 to 8
- frame_count: int32 [4], P('dp'), may hold values from 9 to 16
Outputs:
- grad_inputs: bfloat16 [4, 4, 16, 16, 8, 512], P('pipe', 'dp', 'seq')
- grad_spatial: float32 [4, 9, 512, 512], P('pipe', None, 'seq')
- grad_temporal: float32 [4, 3, 512, 512], P('pipe', None, 'seq')
Inputs may be any that keep to these rules, and one draw needn't show every extreme that they name: For every clip c, frame_count[c] is greater than frame_start[c].
All inputs are finite; a program needn't handle non-finite values.
Results may differ from a plain program's by a relative error of at most 0.02.
Values may be sent and summed in bfloat16 or wider, within the bound.
No kernel may reach another device: no remote copies, remote signals or barrier semaphores. Data moves between devices by JAX's collectives and lax.ppermute only.
A program may use at most 192 MiB of HBM per device.

v0:
```python
import functools

import jax
import jax.numpy as jnp
from jax import lax
from jax.experimental import pallas as pl
from jax.experimental.pallas import tpu as pltpu
from jax.sharding import PartitionSpec as P


F32 = jnp.float32
BF16 = jnp.bfloat16
ANY = pl.BlockSpec(memory_space=pl.ANY)
SMEM = pl.BlockSpec(memory_space=pltpu.SMEM)
VMEM = pl.BlockSpec(memory_space=pltpu.VMEM)

ROWS, COLS, CH = 16, 8, 512
CELLS = ROWS * COLS
FRAMES = 16
CLIPS = 4
SLICE = CH // FRAMES
TAPS = 12
WIDE = TAPS * SLICE
SUB = SLICE // CLIPS


def nn(a, b):
    return lax.dot_general(a, b, (((1,), (0,)), ((), ())), preferred_element_type=F32)


def nt(a, b):
    return lax.dot_general(a, b, (((1,), (1,)), ((), ())), preferred_element_type=F32)


def column_shifts(v):
    col = lax.broadcasted_iota(jnp.int32, v.shape, 0) % COLS
    before = jnp.where(col == 0, 0.0, pltpu.roll(v, 1, 0))
    after = jnp.where(col == COLS - 1, 0.0, pltpu.roll(v, CELLS - 1, 0))
    return {0: v, -1: before, 1: after}


def row_shift(v, step):
    zero = jnp.zeros((COLS, v.shape[1]), v.dtype)
    if step == 0:
        return v
    if step < 0:
        return jnp.concatenate([zero, v[:-COLS]], axis=0)
    return jnp.concatenate([v[COLS:], zero], axis=0)


def forward_kernel(x_ref, wt_ref, ws_ref, mine_ref, slope_ref, wtt_ref, wst_ref):
    x = x_ref[...].astype(F32)
    cols = column_shifts(x)
    pre = None
    for r in range(3):
        for q in range(3):
            term = nn(row_shift(cols[q - 1], r - 1).astype(BF16), ws_ref[3 * r + q])
            pre = term if pre is None else pre + term
    s = jax.nn.sigmoid(pre)
    slope_ref[...] = s * (1.0 + pre * (1.0 - s))
    mine_ref[0] = x.T.astype(BF16)
    mine_ref[1] = (pre * s).astype(BF16).astype(F32).T.astype(BF16)
    for k in range(3):
        wtt_ref[k] = wt_ref[k].T
    for k in range(9):
        wst_ref[k] = ws_ref[k].T


def forward(x, wt, ws):
    return pl.pallas_call(
        forward_kernel,
        name="block_forward",
        out_shape=(
            jax.ShapeDtypeStruct((2, CH, CELLS), BF16),
            jax.ShapeDtypeStruct((CELLS, CH), F32),
            jax.ShapeDtypeStruct((3, CH, CH), BF16),
            jax.ShapeDtypeStruct((9, CH, CH), BF16),
        ),
        in_specs=[VMEM] * 3,
        out_specs=(VMEM,) * 4,
        compiler_params=pltpu.CompilerParams(vmem_limit_bytes=24 << 20),
        cost_estimate=pl.CostEstimate(flops=1208000000, bytes_accessed=13000000, transcendentals=65536),
    )(x, wt, ws)


def cotangents(count, refs):
    start_ref, count_ref = refs[0], refs[1]
    own = refs[2:5]
    got = refs[5 : 5 + count]
    seq = lax.axis_index("seq")
    last = lax.axis_index("pipe") == lax.axis_size("pipe") - 1
    out = []
    for k in range(3):
        t = seq + k
        counted = (t >= start_ref[0]) & (t < count_ref[0])
        if count:
            value = jnp.where(last, own[k][...], got[k][...])
            keep = jnp.where(last, counted, t < FRAMES)
        else:
            value, keep = own[k][...], counted
        out.append(jnp.where(keep, value, jnp.zeros((CELLS, CH), BF16)))
    return out, refs[5 + count :]


def grad_pre_of(cot, slope_ref, wtt_ref):
    grad_act = nn(cot[0], wtt_ref[0]) + nn(cot[1], wtt_ref[1]) + nn(cot[2], wtt_ref[2])
    return (grad_act.astype(BF16).astype(F32) * slope_ref[...]).astype(BF16)


def spread_of(cot, grad_pre, wst_ref):
    cols = column_shifts(grad_pre.astype(F32))
    total = cot.astype(F32)
    for r in range(3):
        for q in range(3):
            lhs = row_shift(cols[1 - q], 1 - r).astype(BF16)
            total = total + nn(lhs, wst_ref[3 * r + q])
    return total.astype(BF16)


def section_kernel(count, *refs):
    cot, (slope_ref, wtt_ref, wst_ref, gin_ref) = cotangents(count, refs)
    grad_pre = grad_pre_of(cot, slope_ref, wtt_ref)
    gin_ref[...] = spread_of(cot[0], grad_pre, wst_ref)


def emit_kernel(count, *refs):
    cot, (slope_ref, wtt_ref, late_ref, cot_ref, pre_ref) = cotangents(count, refs)
    grad_pre = grad_pre_of(cot, slope_ref, wtt_ref)
    late_ref[:, :SLICE] = grad_pre.astype(F32).T.astype(BF16).reshape(FRAMES, SLICE, CELLS)
    late_ref[:, SLICE:] = cot[0].astype(F32).T.astype(BF16).reshape(FRAMES, SLICE, CELLS)
    cot_ref[...] = cot[0]
    pre_ref[...] = grad_pre


def spread_kernel(cot_ref, pre_ref, wst_ref, gin_ref):
    gin_ref[...] = spread_of(cot_ref[...], pre_ref[...], wst_ref)


def small(kernel, outs, args, specs, flops, read):
    return pl.pallas_call(
        kernel,
        out_shape=tuple(jax.ShapeDtypeStruct(o, BF16) for o in outs),
        in_specs=specs,
        out_specs=(VMEM,) * len(outs),
        compiler_params=pltpu.CompilerParams(vmem_limit_bytes=16 << 20),
        cost_estimate=pl.CostEstimate(flops=flops, bytes_accessed=read, transcendentals=0),
    )(*args)


def pack_kernel(*refs):
    pieces, out, sems = refs[:8], refs[8], refs[9]
    copies = [pltpu.make_async_copy(pieces[k], out.at[k], sems.at[k]) for k in range(8)]
    for c in copies:
        c.start()
    for c in copies:
        c.wait()


def pack(pieces):
    return pl.pallas_call(
        pack_kernel,
        name="pack",
        out_shape=jax.ShapeDtypeStruct((8,) + pieces[0].shape, BF16),
        in_specs=[ANY] * 8,
        out_specs=ANY,
        scratch_shapes=[pltpu.SemaphoreType.DMA((8,))],
        compiler_params=pltpu.CompilerParams(vmem_limit_bytes=4 << 20),
        cost_estimate=pl.CostEstimate(flops=0, bytes_accessed=4000000, transcendentals=0),
    )(*pieces)


def weights_kernel(late_ref, *refs):
    ring = refs[:8]
    swapped = refs[8]
    outs = refs[9:13]
    x, act, left, result, sems = refs[13:]
    seq, d = lax.axis_index("seq"), lax.axis_index("dp")
    z, core = seq // 2, seq % 2
    half = FRAMES // 2
    copies = []
    for k in range(half):
        chip = lax.rem(z + k, half)
        for which, source in ((core, ring[k]), (1 - core, swapped.at[k])):
            t = pl.multiple_of((2 * chip + which) * CELLS, CELLS)
            for part, target in ((0, x), (1, act)):
                n = len(copies)
                c = pltpu.make_async_copy(source.at[part], target.at[:, pl.ds(t, CELLS)], sems.at[n])
                c.start()
                copies.append(c)
    g = late_ref[:, :SLICE].astype(F32).reshape(FRAMES * SLICE, CELLS)
    lane = lax.broadcasted_iota(jnp.int32, g.shape, 1)
    row, col = lane // COLS, lane % COLS
    for r in range(3):
        for q in range(3):
            dr, dc = r - 1, q - 1
            v = g if dr == 0 and dc == 0 else pltpu.roll(g, (dr * COLS + dc) % CELLS, 1)
            keep = None
            for at, step, size in ((row, dr, ROWS), (col, dc, COLS)):
                if step:
                    good = (at != 0) if step > 0 else (at != size - 1)
                    keep = good if keep is None else keep & good
            if keep is not None:
                v = jnp.where(keep, v, 0.0)
            v = v.astype(BF16).reshape(FRAMES, SLICE, CELLS)
            base = (3 * r + q) * SLICE
            for f in range(FRAMES):
                left[base : base + SLICE, f * CELLS : (f + 1) * CELLS] = v[f]
    for k in range(3):
        base = (9 + k) * SLICE
        for f in range(FRAMES):
            if f + k < FRAMES:
                v = late_ref[f + k, SLICE:]
            else:
                v = jnp.zeros((SLICE, CELLS), BF16)
            left[base : base + SLICE, f * CELLS : (f + 1) * CELLS] = v
    for c in copies:
        c.wait()
    spatial = nt(x[...], left[: 9 * SLICE])
    temporal = nt(act[...], left[9 * SLICE :])
    result[:, :, :, : 9 * SLICE] = spatial.reshape(FRAMES, CLIPS, SUB, 9 * SLICE)
    result[:, :, :, 9 * SLICE :] = temporal.reshape(FRAMES, CLIPS, SUB, 3 * SLICE)
    for k in range(CLIPS):
        outs[k][...] = result[:, lax.rem(d + k, CLIPS)].astype(BF16)


def weights(late, ring, swapped):
    return pl.pallas_call(
        weights_kernel,
        name="weight_grads",
        out_shape=(jax.ShapeDtypeStruct((FRAMES, SUB, WIDE), BF16),) * CLIPS,
        in_specs=[VMEM] + [ANY] * 9,
        out_specs=(VMEM,) * CLIPS,
        scratch_shapes=[
            pltpu.VMEM((CH, FRAMES * CELLS), BF16),
            pltpu.VMEM((CH, FRAMES * CELLS), BF16),
            pltpu.VMEM((WIDE, FRAMES * CELLS), BF16),
            pltpu.VMEM((FRAMES, CLIPS, SUB, WIDE), F32),
            pltpu.SemaphoreType.DMA((4 * FRAMES // 2,)),
        ],
        compiler_params=pltpu.CompilerParams(vmem_limit_bytes=24 << 20),
        cost_estimate=pl.CostEstimate(flops=1610000000, bytes_accessed=5000000, transcendentals=0),
    )(late, *ring, swapped)


def assemble_kernel(*refs):
    parts, (spatial_ref, temporal_ref) = refs[:CLIPS], refs[CLIPS:]
    d = lax.axis_index("dp")
    for k in range(CLIPS):
        source = lax.rem(d + CLIPS - k, CLIPS)
        rows = pl.ds(pl.multiple_of(source * SUB, SUB), SUB)
        part = parts[k][...].astype(F32)
        for tap in range(TAPS):
            line = jnp.concatenate(
                [part[s, :, tap * SLICE : (tap + 1) * SLICE] for s in range(FRAMES)], axis=-1
            )
            if tap < 9:
                spatial_ref[tap, rows, :] = line
            else:
                temporal_ref[tap - 9, rows, :] = line


def assemble(parts):
    return pl.pallas_call(
        assemble_kernel,
        name="assemble",
        out_shape=(
            jax.ShapeDtypeStruct((9, SLICE, CH), F32),
            jax.ShapeDtypeStruct((3, SLICE, CH), F32),
        ),
        in_specs=[VMEM] * CLIPS,
        out_specs=(VMEM, VMEM),
        compiler_params=pltpu.CompilerParams(vmem_limit_bytes=24 << 20),
        cost_estimate=pl.CostEstimate(flops=1000000, bytes_accessed=1200000, transcendentals=0),
    )(*parts)


def send(value, axes, sizes, step):
    n, m = sizes
    pairs = [
        (a * m + b, (a + step[0]) % n * m + (b + step[1]) % m) for a in range(n) for b in range(m)
    ]
    return lax.ppermute(value, axes, pairs)


def around(value, axis, size, step):
    return lax.ppermute(value, axis, [(i, (i + step) % size) for i in range(size)])


def local(sizes, *args):
    return backward(sizes, *args)


def backward(sizes, section_inputs, w_spatial, w_temporal, grad_output, frame_start, frame_count):
    axes = ("pipe", "seq")
    steps = sizes[0]
    x = section_inputs.reshape(CELLS, CH)
    ws, wt = w_spatial[0], w_temporal[0]
    cot = grad_output.reshape(CELLS, CH)
    ahead2 = send(cot, axes, sizes, (0, -2))
    ahead1 = send(cot, axes, sizes, (0, -1))
    mine, slope, wtt, wst = forward(x, wt, ws)
    head = [frame_start, frame_count, cot, ahead1, ahead2]
    head_specs = [SMEM, SMEM] + [VMEM] * 3
    ring = {0: mine}
    half = FRAMES // 2

    def grow(k):
        ring[-k] = around(ring[1 - k], "seq", FRAMES, 2)
        if k < half // 2:
            ring[k] = around(ring[k - 1], "seq", FRAMES, -2)

    grow(1)
    got = []
    for step in range(steps - 1):
        (grad_in,) = small(
            functools.partial(section_kernel, len(got)),
            [(CELLS, CH)],
            head + got + [slope, wtt, wst],
            head_specs + [VMEM] * (len(got) + 3),
            805000000,
            7000000,
        )
        got = [send(grad_in, axes, sizes, (-1, -k)) for k in (2, 1, 0)][::-1]
        grow(step + 2)
    late, cot0, grad_pre = small(
        functools.partial(emit_kernel, len(got)),
        [(FRAMES, 2 * SLICE, CELLS), (CELLS, CH), (CELLS, CH)],
        head + got + [slope, wtt],
        head_specs + [VMEM] * (len(got) + 2),
        200000000,
        2000000,
    )
    gathered = lax.all_to_all(late, "seq", 0, 0, tiled=True)
    pieces = [ring[k if k < half // 2 else k - half] for k in range(half)]
    packed = pack(pieces)
    swapped = lax.ppermute(packed, "seq", [(i, i ^ 1) for i in range(FRAMES)])
    (grad_in,) = small(
        spread_kernel, [(CELLS, CH)], [cot0, grad_pre, wst], [VMEM] * 3, 604000000, 5000000
    )
    partial = weights(gathered, pieces, swapped)
    shares = [partial[0]] + [around(partial[k], "dp", CLIPS, k) for k in (1, 2, 3)]
    share = sum(s.astype(F32) for s in shares).astype(BF16)
    share = lax.all_to_all(share, "seq", 0, 0, tiled=True)
    parts = [share] + [around(share, "dp", CLIPS, k) for k in (1, 2, 3)]
    spatial, temporal = assemble(parts)
    return grad_in.reshape(section_inputs.shape), spatial[None], temporal[None]


def solution(mesh):
    sizes = (mesh.shape["pipe"], mesh.shape["seq"])
    placed = (
        P("pipe", "dp", "seq", None, None, None),
        P("pipe", None, None, None),
        P("pipe", None, None, None),
        P("dp", "seq", None, None, None),
        P("dp"),
        P("dp"),
    )
    return jax.shard_map(
        functools.partial(local, sizes),
        mesh=mesh,
        in_specs=placed,
        out_specs=(
            P("pipe", "dp", "seq", None, None, None),
            P("pipe", None, "seq", None),
            P("pipe", None, "seq", None),
        ),
        check_vma=False,
    )
```

profile of v0, /device:TPU:1, one launch (start us, length us, event | category | flops | bytes accessed | tf_op | source)
XLA Modules:
  0.0 145.0 jit_solution(3425702316368503206)
XLA Ops:
  0.6 2.3 %copy-done = bf16[1,9,512,512]{3,2,1,0:T(8,128)(2,1)S(1)} copy-done((bf16[1,9,512,512]{3,2,1,0:T(8,128)(2,1)S(1)}, bf16[1,9,512,512]{3,2,1,0:T(8,128)(2,1)}, u32[]{:S(2)}) %copy-start) | copy-done | bytes 4718616
  5.3 1.9 %block_forward.1 = (bf16[2,512,128]{2,1,0:T(8,128)(2,1)S(1)}, f32[128,512]{1,0:T(8,128)S(1)}, bf16[3,512,512]{2,1,0:T(8,128)(2,1)S(1)}, bf16[9,512,512]{2,1,0:T(8,128)(2,1)S(1)}) custom-call(bf16[128,512]{1,0:T(8,128)(2,1)S(1)} %bitcast.15, bf16[3,512,512]{2,1,0:T(8,128)(2,1)S(1)} %bitcast.14, bf16[9,512,512]{2,1,0:T(8,128)(2,1)S(1)} %bitcast.7), custom_call_target="tpu_custom_call" | custom-call | flops 1208000000 | bytes 13000000 | tf_op jit(solution)/shard_map/block_forward/pallas_call | solution.py:70
  7.2 2.5 %collective-permute-start.14 = (bf16[2,512,128]{2,1,0:T(8,128)(2,1)S(1)}, bf16[2,512,128]{2,1,0:T(8,128)(2,1)S(1)}, u32[]{:S(2)}, u32[]{:S(2)}) collective-permute-start(bf16[2,512,128]{2,1,0:T(8,128)(2,1)S(1)} %get-tuple-element.22.refs_0_), channel_id=1, source_target_pairs={{0,8},{4,12},{8,16},{12,20},{16,24},{20,28},{24,32},{28,36},{32,40... | collective-permute-start | bytes 786440 | tf_op jit(solution)/shard_map/ppermute | solution.py:286
  9.7 4.0 %collective-permute-start.11 = (bf16[2,512,128]{2,1,0:T(8,128)(2,1)S(1)}, bf16[2,512,128]{2,1,0:T(8,128)(2,1)S(1)}, u32[]{:S(2)}, u32[]{:S(2)}) collective-permute-start(bf16[2,512,128]{2,1,0:T(8,128)(2,1)S(1)} %get-tuple-element.22.refs_0_), channel_id=1, source_target_pairs={{0,56},{4,60},{8,0},{12,4},{16,8},{20,12},{24,16},{28,20},{32,24},... | collective-permute-start | bytes 786440 | tf_op jit(solution)/shard_map/ppermute | solution.py:286
  13.7 5.9 %collective-permute-done.14.refs_7_ = bf16[2,512,128]{2,1,0:T(8,128)(2,1)S(1)} collective-permute-done((bf16[2,512,128]{2,1,0:T(8,128)(2,1)S(1)}, bf16[2,512,128]{2,1,0:T(8,128)(2,1)S(1)}, u32[]{:S(2)}, u32[]{:S(2)}) %collective-permute-start.14) | collective-permute-done | bytes 262176 | tf_op jit(solution)/shard_map/ppermute | solution.py:286
  19.6 2.7 %collective-permute-start.12 = (bf16[2,512,128]{2,1,0:T(8,128)(2,1)S(1)}, bf16[2,512,128]{2,1,0:T(8,128)(2,1)S(1)}, u32[]{:S(2)}, u32[]{:S(2)}) collective-permute-start(bf16[2,512,128]{2,1,0:T(8,128)(2,1)S(1)} %collective-permute-done.11.refs_1_), channel_id=1, source_target_pairs={{0,56},{4,60},{8,0},{12,4},{16,8},{20,12},{24,16},{28,20},{32,24},... | collective-permute-start | bytes 786440 | tf_op jit(solution)/shard_map/ppermute | solution.py:286
  22.3 5.1 %collective-permute-done.15.refs_6_ = bf16[2,512,128]{2,1,0:T(8,128)(2,1)S(1)} collective-permute-done((bf16[2,512,128]{2,1,0:T(8,128)(2,1)S(1)}, bf16[2,512,128]{2,1,0:T(8,128)(2,1)S(1)}, u32[]{:S(2)}, u32[]{:S(2)}) %collective-permute-start.15) | collective-permute-done | bytes 262176 | tf_op jit(solution)/shard_map/ppermute | solution.py:286
  27.5 2.7 %collective-permute-start.13 = (bf16[2,512,128]{2,1,0:T(8,128)(2,1)S(1)}, bf16[2,512,128]{2,1,0:T(8,128)(2,1)S(1)}, u32[]{:S(2)}, u32[]{:S(2)}) collective-permute-start(bf16[2,512,128]{2,1,0:T(8,128)(2,1)S(1)} %collective-permute-done.12.refs_2_), channel_id=1, source_target_pairs={{0,56},{4,60},{8,0},{12,4},{16,8},{20,12},{24,16},{28,20},{32,24},... | collective-permute-start | bytes 786440 | tf_op jit(solution)/shard_map/ppermute | solution.py:286
  30.1 4.3 %collective-permute-done.16.refs_5_ = bf16[2,512,128]{2,1,0:T(8,128)(2,1)S(1)} collective-permute-done((bf16[2,512,128]{2,1,0:T(8,128)(2,1)S(1)}, bf16[2,512,128]{2,1,0:T(8,128)(2,1)S(1)}, u32[]{:S(2)}, u32[]{:S(2)}) %collective-permute-start.16) | collective-permute-done | bytes 262176 | tf_op jit(solution)/shard_map/ppermute | solution.py:286
  34.4 6.4 %collective-permute-done.17.refs_4_ = bf16[2,512,128]{2,1,0:T(8,128)(2,1)S(1)} collective-permute-done((bf16[2,512,128]{2,1,0:T(8,128)(2,1)S(1)}, bf16[2,512,128]{2,1,0:T(8,128)(2,1)S(1)}, u32[]{:S(2)}, u32[]{:S(2)}) %collective-permute-start.17) | collective-permute-done | bytes 262176 | tf_op jit(solution)/shard_map/ppermute | solution.py:286
  41.1 4.2 %collective-permute-start.18 = (bf16[8,2,512,128]{3,2,1,0:T(8,128)(2,1)S(1)}, bf16[8,2,512,128]{3,2,1,0:T(8,128)(2,1)S(1)}, u32[]{:S(2)}, u32[]{:S(2)}) collective-permute-start(bf16[8,2,512,128]{3,2,1,0:T(8,128)(2,1)S(1)} %pack.1), channel_id=1, source_target_pairs={{0,4},{4,0},{8,12},{12,8},{16,20},{20,16},{24,28},{28,24},{32,36},... | collective-permute-start | bytes 6291464 | tf_op jit(solution)/shard_map/ppermute | solution.py:336
  46.7 3.5 %collective-permute-done.1.refs_4_ = bf16[128,512]{1,0:T(8,128)(2,1)S(1)} collective-permute-done((bf16[128,512]{1,0:T(8,128)(2,1)S(1)}, bf16[128,512]{1,0:T(8,128)(2,1)S(1)}, u32[]{:S(2)}, u32[]{:S(2)}) %collective-permute-start.1) | collective-permute-done | bytes 131104 | tf_op jit(solution)/shard_map/ppermute | solution.py:282
  50.3 1.7 %collective-permute-done.refs_3_ = bf16[128,512]{1,0:T(8,128)(2,1)S(1)} collective-permute-done((bf16[128,512]{1,0:T(8,128)(2,1)S(1)}, bf16[128,512]{1,0:T(8,128)(2,1)S(1)}, u32[]{:S(2)}, u32[]{:S(2)}) %collective-permute-start) | collective-permute-done | bytes 131104 | tf_op jit(solution)/shard_map/ppermute | solution.py:282
  53.1 3.8 %collective-permute-start.4 = (bf16[128,512]{1,0:T(8,128)(2,1)S(1)}, bf16[128,512]{1,0:T(8,128)(2,1)S(1)}, u32[]{:S(2)}, u32[]{:S(2)}) collective-permute-start(bf16[128,512]{1,0:T(8,128)(2,1)S(1)} %shard_map.85), channel_id=1, source_target_pairs={{0,248},{4,252},{8,192},{12,196},{16,200},{20,204},{24,208},{28,21... | collective-permute-start | bytes 393224 | tf_op jit(solution)/shard_map/ppermute | solution.py:282
  57.3 2.9 %collective-permute-done.4.refs_7_ = bf16[128,512]{1,0:T(8,128)(2,1)S(1)} collective-permute-done((bf16[128,512]{1,0:T(8,128)(2,1)S(1)}, bf16[128,512]{1,0:T(8,128)(2,1)S(1)}, u32[]{:S(2)}, u32[]{:S(2)}) %collective-permute-start.4) | collective-permute-done | bytes 131104 | tf_op jit(solution)/shard_map/ppermute | solution.py:282
  60.2 3.8 %collective-permute-done.3.refs_6_ = bf16[128,512]{1,0:T(8,128)(2,1)S(1)} collective-permute-done((bf16[128,512]{1,0:T(8,128)(2,1)S(1)}, bf16[128,512]{1,0:T(8,128)(2,1)S(1)}, u32[]{:S(2)}, u32[]{:S(2)}) %collective-permute-start.3) | collective-permute-done | bytes 131104 | tf_op jit(solution)/shard_map/ppermute | solution.py:282
  66.7 2.8 %collective-permute-start.7 = (bf16[128,512]{1,0:T(8,128)(2,1)S(1)}, bf16[128,512]{1,0:T(8,128)(2,1)S(1)}, u32[]{:S(2)}, u32[]{:S(2)}) collective-permute-start(bf16[128,512]{1,0:T(8,128)(2,1)S(1)} %shard_map.86), channel_id=1, source_target_pairs={{0,248},{4,252},{8,192},{12,196},{16,200},{20,204},{24,208},{28,21... | collective-permute-start | bytes 393224 | tf_op jit(solution)/shard_map/ppermute | solution.py:282
  70.9 2.2 %collective-permute-done.7.refs_7_ = bf16[128,512]{1,0:T(8,128)(2,1)S(1)} collective-permute-done((bf16[128,512]{1,0:T(8,128)(2,1)S(1)}, bf16[128,512]{1,0:T(8,128)(2,1)S(1)}, u32[]{:S(2)}, u32[]{:S(2)}) %collective-permute-start.7) | collective-permute-done | bytes 131104 | tf_op jit(solution)/shard_map/ppermute | solution.py:282
  73.1 3.4 %collective-permute-done.6.refs_6_ = bf16[128,512]{1,0:T(8,128)(2,1)S(1)} collective-permute-done((bf16[128,512]{1,0:T(8,128)(2,1)S(1)}, bf16[128,512]{1,0:T(8,128)(2,1)S(1)}, u32[]{:S(2)}, u32[]{:S(2)}) %collective-permute-start.6) | collective-permute-done | bytes 131104 | tf_op jit(solution)/shard_map/ppermute | solution.py:282
  76.5 2.3 %collective-permute-done.5.refs_5_ = bf16[128,512]{1,0:T(8,128)(2,1)S(1)} collective-permute-done((bf16[128,512]{1,0:T(8,128)(2,1)S(1)}, bf16[128,512]{1,0:T(8,128)(2,1)S(1)}, u32[]{:S(2)}, u32[]{:S(2)}) %collective-permute-start.5) | collective-permute-done | bytes 131104 | tf_op jit(solution)/shard_map/ppermute | solution.py:282
  80.0 3.9 %collective-permute-start.10 = (bf16[128,512]{1,0:T(8,128)(2,1)S(1)}, bf16[128,512]{1,0:T(8,128)(2,1)S(1)}, u32[]{:S(2)}, u32[]{:S(2)}) collective-permute-start(bf16[128,512]{1,0:T(8,128)(2,1)S(1)} %shard_map.87), channel_id=1, source_target_pairs={{0,248},{4,252},{8,192},{12,196},{16,200},{20,204},{24,208},{28,21... | collective-permute-start | bytes 393224 | tf_op jit(solution)/shard_map/ppermute | solution.py:282
  84.0 2.4 %collective-permute-done.10.refs_7_ = bf16[128,512]{1,0:T(8,128)(2,1)S(1)} collective-permute-done((bf16[128,512]{1,0:T(8,128)(2,1)S(1)}, bf16[128,512]{1,0:T(8,128)(2,1)S(1)}, u32[]{:S(2)}, u32[]{:S(2)}) %collective-permute-start.10) | collective-permute-done | bytes 131104 | tf_op jit(solution)/shard_map/ppermute | solution.py:282
  86.4 4.8 %collective-permute-done.9.refs_6_ = bf16[128,512]{1,0:T(8,128)(2,1)S(1)} collective-permute-done((bf16[128,512]{1,0:T(8,128)(2,1)S(1)}, bf16[128,512]{1,0:T(8,128)(2,1)S(1)}, u32[]{:S(2)}, u32[]{:S(2)}) %collective-permute-start.9) | collective-permute-done | bytes 131104 | tf_op jit(solution)/shard_map/ppermute | solution.py:282
  91.2 1.7 %collective-permute-done.8.refs_5_ = bf16[128,512]{1,0:T(8,128)(2,1)S(1)} collective-permute-done((bf16[128,512]{1,0:T(8,128)(2,1)S(1)}, bf16[128,512]{1,0:T(8,128)(2,1)S(1)}, u32[]{:S(2)}, u32[]{:S(2)}) %collective-permute-start.8) | collective-permute-done | bytes 131104 | tf_op jit(solution)/shard_map/ppermute | solution.py:282
  93.4 15.5 %all_to_all.10.late_ref = bf16[16,64,128]{2,1,0:T(8,128)(2,1)S(1)} all-to-all(bf16[16,64,128]{2,1,0:T(8,128)(2,1)S(1)} %get-tuple-element.21), channel_id=1, replica_groups=mesh['pipe'=4,'seq'=16,'dp'=4] {'seq'}, dimensions={0} | all-to-all | bytes 524288 | tf_op jit(solution)/shard_map/all_to_all | solution.py:333
  108.9 3.9 %weight_grads.1 = (bf16[16,8,384]{2,1,0:T(8,128)(2,1)S(1)}, bf16[16,8,384]{2,1,0:T(8,128)(2,1)S(1)}, bf16[16,8,384]{2,1,0:T(8,128)(2,1)S(1)}, bf16[16,8,384]{2,1,0:T(8,128)(2,1)S(1)}) custom-call(bf16[16,64,128]{2,1,0:T(8,128)(2,1)S(1)} %all_to_all.10.late_ref, bf16[2,512,128]{2,1,0:T(8,128)(2,1)S(1)} %get-tuple-element.22.refs_0_, ...), custom_call_target="tpu_custom_call" | custom-call | flops 1610000000 | bytes 5000000 | tf_op jit(solution)/shard_map/weight_grads/pallas_call | solution.py:227
  114.2 2.5 %collective-permute-start.20 = (bf16[16,8,384]{2,1,0:T(8,128)(2,1)S(1)}, bf16[16,8,384]{2,1,0:T(8,128)(2,1)S(1)}, u32[]{:S(2)}, u32[]{:S(2)}) collective-permute-start(bf16[16,8,384]{2,1,0:T(8,128)(2,1)S(1)} %get-tuple-element.25), channel_id=1, source_target_pairs={{0,2},{1,3},{2,0},{3,1},{4,6},{5,7},{6,4},{7,5},{8,10},{9,11},{10,... | collective-permute-start | bytes 294920 | tf_op jit(solution)/shard_map/ppermute | solution.py:286
  118.8 3.1 %collective-permute-done.20 = bf16[16,8,384]{2,1,0:T(8,128)(2,1)S(1)} collective-permute-done((bf16[16,8,384]{2,1,0:T(8,128)(2,1)S(1)}, bf16[16,8,384]{2,1,0:T(8,128)(2,1)S(1)}, u32[]{:S(2)}, u32[]{:S(2)}) %collective-permute-start.20) | collective-permute-done | bytes 98336 | tf_op jit(solution)/shard_map/ppermute | solution.py:286
  122.1 11.4 %all_to_all.11.refs_0_ = bf16[16,8,384]{2,1,0:T(8,128)(2,1)S(1)} all-to-all(bf16[16,8,384]{2,1,0:T(8,128)(2,1)S(1)} %add_convert_fusion), channel_id=1, replica_groups=mesh['pipe'=4,'seq'=16,'dp'=4] {'seq'}, dimensions={0} | all-to-all | bytes 196608 | tf_op jit(solution)/shard_map/all_to_all | solution.py:343
  133.5 2.0 %collective-permute-start.24 = (bf16[16,8,384]{2,1,0:T(8,128)(2,1)S(1)}, bf16[16,8,384]{2,1,0:T(8,128)(2,1)S(1)}, u32[]{:S(2)}, u32[]{:S(2)}) collective-permute-start(bf16[16,8,384]{2,1,0:T(8,128)(2,1)S(1)} %all_to_all.11.refs_0_), channel_id=1, source_target_pairs={{0,3},{1,0},{2,1},{3,2},{4,7},{5,4},{6,5},{7,6},{8,11},{9,8},{10,9... | collective-permute-start | bytes 294920 | tf_op jit(solution)/shard_map/ppermute | solution.py:286
  138.1 3.0 %collective-permute-done.23.refs_2_ = bf16[16,8,384]{2,1,0:T(8,128)(2,1)S(1)} collective-permute-done((bf16[16,8,384]{2,1,0:T(8,128)(2,1)S(1)}, bf16[16,8,384]{2,1,0:T(8,128)(2,1)S(1)}, u32[]{:S(2)}, u32[]{:S(2)}) %collective-permute-start.23) | collective-permute-done | bytes 98336 | tf_op jit(solution)/shard_map/ppermute | solution.py:286
  141.1 2.7 %collective-permute-done.22.refs_1_ = bf16[16,8,384]{2,1,0:T(8,128)(2,1)S(1)} collective-permute-done((bf16[16,8,384]{2,1,0:T(8,128)(2,1)S(1)}, bf16[16,8,384]{2,1,0:T(8,128)(2,1)S(1)}, u32[]{:S(2)}, u32[]{:S(2)}) %collective-permute-start.22) | collective-permute-done | bytes 98336 | tf_op jit(solution)/shard_map/ppermute | solution.py:286
  (38 shorter events, 17.5 us)
Async XLA Ops:
  0.6 2.3 %copy-start = (bf16[1,9,512,512]{3,2,1,0:T(8,128)(2,1)S(1)}, bf16[1,9,512,512]{3,2,1,0:T(8,128)(2,1)}, u32[]{:S(2)}) copy-start(bf16[1,9,512,512]{3,2,1,0:T(8,128)(2,1)} %param.7) | copy-start | bytes 14155780
  3.0 1.4 copy-start.2
  4.4 0.9 copy-start.3
  7.2 38.1 %copy-start.1 = (bf16[1,1,16,8,512]{4,3,2,1,0:T(8,128)(2,1)S(1)}, bf16[1,1,16,8,512]{4,3,2,1,0:T(8,128)(2,1)}, u32[]{:S(2)}) copy-start(bf16[1,1,16,8,512]{4,3,2,1,0:T(8,128)(2,1)} %param.9) | copy-start | bytes 393220
  7.2 12.5 %collective-permute-start.14 = (bf16[2,512,128]{2,1,0:T(8,128)(2,1)S(1)}, bf16[2,512,128]{2,1,0:T(8,128)(2,1)S(1)}, u32[]{:S(2)}, u32[]{:S(2)}) collective-permute-start(bf16[2,512,128]{2,1,0:T(8,128)(2,1)S(1)} %get-tuple-element.22.refs_0_), channel_id=1, source_target_pairs={{0,8},{4,12},{8,16},{12,20},{16,24},{20,28},{24,32},{28,36},{32,40... | collective-permute-start | bytes 786440 | tf_op jit(solution)/shard_map/ppermute | solution.py:286
  9.7 9.9 %collective-permute-start.11 = (bf16[2,512,128]{2,1,0:T(8,128)(2,1)S(1)}, bf16[2,512,128]{2,1,0:T(8,128)(2,1)S(1)}, u32[]{:S(2)}, u32[]{:S(2)}) collective-permute-start(bf16[2,512,128]{2,1,0:T(8,128)(2,1)S(1)} %get-tuple-element.22.refs_0_), channel_id=1, source_target_pairs={{0,56},{4,60},{8,0},{12,4},{16,8},{20,12},{24,16},{28,20},{32,24},... | collective-permute-start | bytes 786440 | tf_op jit(solution)/shard_map/ppermute | solution.py:286
  19.6 7.8 %collective-permute-start.15 = (bf16[2,512,128]{2,1,0:T(8,128)(2,1)S(1)}, bf16[2,512,128]{2,1,0:T(8,128)(2,1)S(1)}, u32[]{:S(2)}, u32[]{:S(2)}) collective-permute-start(bf16[2,512,128]{2,1,0:T(8,128)(2,1)S(1)} %collective-permute-done.14.refs_7_), channel_id=1, source_target_pairs={{0,8},{4,12},{8,16},{12,20},{16,24},{20,28},{24,32},{28,36},{32,40... | collective-permute-start | bytes 786440 | tf_op jit(solution)/shard_map/ppermute | solution.py:286
  19.6 7.8 %collective-permute-start.12 = (bf16[2,512,128]{2,1,0:T(8,128)(2,1)S(1)}, bf16[2,512,128]{2,1,0:T(8,128)(2,1)S(1)}, u32[]{:S(2)}, u32[]{:S(2)}) collective-permute-start(bf16[2,512,128]{2,1,0:T(8,128)(2,1)S(1)} %collective-permute-done.11.refs_1_), channel_id=1, source_target_pairs={{0,56},{4,60},{8,0},{12,4},{16,8},{20,12},{24,16},{28,20},{32,24},... | collective-permute-start | bytes 786440 | tf_op jit(solution)/shard_map/ppermute | solution.py:286
  27.5 7.0 %collective-permute-start.16 = (bf16[2,512,128]{2,1,0:T(8,128)(2,1)S(1)}, bf16[2,512,128]{2,1,0:T(8,128)(2,1)S(1)}, u32[]{:S(2)}, u32[]{:S(2)}) collective-permute-start(bf16[2,512,128]{2,1,0:T(8,128)(2,1)S(1)} %collective-permute-done.15.refs_6_), channel_id=1, source_target_pairs={{0,8},{4,12},{8,16},{12,20},{16,24},{20,28},{24,32},{28,36},{32,40... | collective-permute-start | bytes 786440 | tf_op jit(solution)/shard_map/ppermute | solution.py:286
  27.5 7.0 %collective-permute-start.13 = (bf16[2,512,128]{2,1,0:T(8,128)(2,1)S(1)}, bf16[2,512,128]{2,1,0:T(8,128)(2,1)S(1)}, u32[]{:S(2)}, u32[]{:S(2)}) collective-permute-start(bf16[2,512,128]{2,1,0:T(8,128)(2,1)S(1)} %collective-permute-done.12.refs_2_), channel_id=1, source_target_pairs={{0,56},{4,60},{8,0},{12,4},{16,8},{20,12},{24,16},{28,20},{32,24},... | collective-permute-start | bytes 786440 | tf_op jit(solution)/shard_map/ppermute | solution.py:286
  34.4 6.4 %collective-permute-start.17 = (bf16[2,512,128]{2,1,0:T(8,128)(2,1)S(1)}, bf16[2,512,128]{2,1,0:T(8,128)(2,1)S(1)}, u32[]{:S(2)}, u32[]{:S(2)}) collective-permute-start(bf16[2,512,128]{2,1,0:T(8,128)(2,1)S(1)} %collective-permute-done.16.refs_5_), channel_id=1, source_target_pairs={{0,8},{4,12},{8,16},{12,20},{16,24},{20,28},{24,32},{28,36},{32,40... | collective-permute-start | bytes 786440 | tf_op jit(solution)/shard_map/ppermute | solution.py:286
  41.1 67.8 %collective-permute-start.18 = (bf16[8,2,512,128]{3,2,1,0:T(8,128)(2,1)S(1)}, bf16[8,2,512,128]{3,2,1,0:T(8,128)(2,1)S(1)}, u32[]{:S(2)}, u32[]{:S(2)}) collective-permute-start(bf16[8,2,512,128]{3,2,1,0:T(8,128)(2,1)S(1)} %pack.1), channel_id=1, source_target_pairs={{0,4},{4,0},{8,12},{12,8},{16,20},{20,16},{24,28},{28,24},{32,36},... | collective-permute-start | bytes 6291464 | tf_op jit(solution)/shard_map/ppermute | solution.py:336
  45.3 5.0 %collective-permute-start.1 = (bf16[128,512]{1,0:T(8,128)(2,1)S(1)}, bf16[128,512]{1,0:T(8,128)(2,1)S(1)}, u32[]{:S(2)}, u32[]{:S(2)}) collective-permute-start(bf16[128,512]{1,0:T(8,128)(2,1)S(1)} %bitcast.8), channel_id=1, source_target_pairs={{0,56},{4,60},{8,0},{12,4},{16,8},{20,12},{24,16},{28,20},{32,24},... | collective-permute-start | bytes 393224 | tf_op jit(solution)/shard_map/ppermute | solution.py:282
  45.3 6.6 %collective-permute-start = (bf16[128,512]{1,0:T(8,128)(2,1)S(1)}, bf16[128,512]{1,0:T(8,128)(2,1)S(1)}, u32[]{:S(2)}, u32[]{:S(2)}) collective-permute-start(bf16[128,512]{1,0:T(8,128)(2,1)S(1)} %bitcast.9), channel_id=1, source_target_pairs={{0,60},{4,0},{8,4},{12,8},{16,12},{20,16},{24,20},{28,24},{32,28},... | collective-permute-start | bytes 393224 | tf_op jit(solution)/shard_map/ppermute | solution.py:282
  53.1 7.1 %collective-permute-start.4 = (bf16[128,512]{1,0:T(8,128)(2,1)S(1)}, bf16[128,512]{1,0:T(8,128)(2,1)S(1)}, u32[]{:S(2)}, u32[]{:S(2)}) collective-permute-start(bf16[128,512]{1,0:T(8,128)(2,1)S(1)} %shard_map.85), channel_id=1, source_target_pairs={{0,248},{4,252},{8,192},{12,196},{16,200},{20,204},{24,208},{28,21... | collective-permute-start | bytes 393224 | tf_op jit(solution)/shard_map/ppermute | solution.py:282
  56.9 7.1 %collective-permute-start.3 = (bf16[128,512]{1,0:T(8,128)(2,1)S(1)}, bf16[128,512]{1,0:T(8,128)(2,1)S(1)}, u32[]{:S(2)}, u32[]{:S(2)}) collective-permute-start(bf16[128,512]{1,0:T(8,128)(2,1)S(1)} %shard_map.85), channel_id=1, source_target_pairs={{0,252},{4,192},{8,196},{12,200},{16,204},{20,208},{24,212},{28,21... | collective-permute-start | bytes 393224 | tf_op jit(solution)/shard_map/ppermute | solution.py:282
  56.9 8.6 %collective-permute-start.2 = (bf16[128,512]{1,0:T(8,128)(2,1)S(1)}, bf16[128,512]{1,0:T(8,128)(2,1)S(1)}, u32[]{:S(2)}, u32[]{:S(2)}) collective-permute-start(bf16[128,512]{1,0:T(8,128)(2,1)S(1)} %shard_map.85), channel_id=1, source_target_pairs={{0,192},{4,196},{8,200},{12,204},{16,208},{20,212},{24,216},{28,22... | collective-permute-start | bytes 393224 | tf_op jit(solution)/shard_map/ppermute | solution.py:282
  66.7 6.4 %collective-permute-start.7 = (bf16[128,512]{1,0:T(8,128)(2,1)S(1)}, bf16[128,512]{1,0:T(8,128)(2,1)S(1)}, u32[]{:S(2)}, u32[]{:S(2)}) collective-permute-start(bf16[128,512]{1,0:T(8,128)(2,1)S(1)} %shard_map.86), channel_id=1, source_target_pairs={{0,248},{4,252},{8,192},{12,196},{16,200},{20,204},{24,208},{28,21... | collective-permute-start | bytes 393224 | tf_op jit(solution)/shard_map/ppermute | solution.py:282
  69.5 7.0 %collective-permute-start.6 = (bf16[128,512]{1,0:T(8,128)(2,1)S(1)}, bf16[128,512]{1,0:T(8,128)(2,1)S(1)}, u32[]{:S(2)}, u32[]{:S(2)}) collective-permute-start(bf16[128,512]{1,0:T(8,128)(2,1)S(1)} %shard_map.86), channel_id=1, source_target_pairs={{0,252},{4,192},{8,196},{12,200},{16,204},{20,208},{24,212},{28,21... | collective-permute-start | bytes 393224 | tf_op jit(solution)/shard_map/ppermute | solution.py:282
  69.9 8.9 %collective-permute-start.5 = (bf16[128,512]{1,0:T(8,128)(2,1)S(1)}, bf16[128,512]{1,0:T(8,128)(2,1)S(1)}, u32[]{:S(2)}, u32[]{:S(2)}) collective-permute-start(bf16[128,512]{1,0:T(8,128)(2,1)S(1)} %shard_map.86), channel_id=1, source_target_pairs={{0,192},{4,196},{8,200},{12,204},{16,208},{20,212},{24,216},{28,22... | collective-permute-start | bytes 393224 | tf_op jit(solution)/shard_map/ppermute | solution.py:282
  80.0 6.4 %collective-permute-start.10 = (bf16[128,512]{1,0:T(8,128)(2,1)S(1)}, bf16[128,512]{1,0:T(8,128)(2,1)S(1)}, u32[]{:S(2)}, u32[]{:S(2)}) collective-permute-start(bf16[128,512]{1,0:T(8,128)(2,1)S(1)} %shard_map.87), channel_id=1, source_target_pairs={{0,248},{4,252},{8,192},{12,196},{16,200},{20,204},{24,208},{28,21... | collective-permute-start | bytes 393224 | tf_op jit(solution)/shard_map/ppermute | solution.py:282
  83.9 7.2 %collective-permute-start.9 = (bf16[128,512]{1,0:T(8,128)(2,1)S(1)}, bf16[128,512]{1,0:T(8,128)(2,1)S(1)}, u32[]{:S(2)}, u32[]{:S(2)}) collective-permute-start(bf16[128,512]{1,0:T(8,128)(2,1)S(1)} %shard_map.87), channel_id=1, source_target_pairs={{0,252},{4,192},{8,196},{12,200},{16,204},{20,208},{24,212},{28,21... | collective-permute-start | bytes 393224 | tf_op jit(solution)/shard_map/ppermute | solution.py:282
  84.0 8.9 %collective-permute-start.8 = (bf16[128,512]{1,0:T(8,128)(2,1)S(1)}, bf16[128,512]{1,0:T(8,128)(2,1)S(1)}, u32[]{:S(2)}, u32[]{:S(2)}) collective-permute-start(bf16[128,512]{1,0:T(8,128)(2,1)S(1)} %shard_map.87), channel_id=1, source_target_pairs={{0,192},{4,196},{8,200},{12,204},{16,208},{20,212},{24,216},{28,22... | collective-permute-start | bytes 393224 | tf_op jit(solution)/shard_map/ppermute | solution.py:282
  112.9 6.0 %collective-permute-start.19 = (bf16[16,8,384]{2,1,0:T(8,128)(2,1)S(1)}, bf16[16,8,384]{2,1,0:T(8,128)(2,1)S(1)}, u32[]{:S(2)}, u32[]{:S(2)}) collective-permute-start(bf16[16,8,384]{2,1,0:T(8,128)(2,1)S(1)} %get-tuple-element.24), channel_id=1, source_target_pairs={{0,1},{1,2},{2,3},{3,0},{4,5},{5,6},{6,7},{7,4},{8,9},{9,10},{10,1... | collective-permute-start | bytes 294920 | tf_op jit(solution)/shard_map/ppermute | solution.py:286
  114.2 7.8 %collective-permute-start.20 = (bf16[16,8,384]{2,1,0:T(8,128)(2,1)S(1)}, bf16[16,8,384]{2,1,0:T(8,128)(2,1)S(1)}, u32[]{:S(2)}, u32[]{:S(2)}) collective-permute-start(bf16[16,8,384]{2,1,0:T(8,128)(2,1)S(1)} %get-tuple-element.25), channel_id=1, source_target_pairs={{0,2},{1,3},{2,0},{3,1},{4,6},{5,7},{6,4},{7,5},{8,10},{9,11},{10,... | collective-permute-start | bytes 294920 | tf_op jit(solution)/shard_map/ppermute | solution.py:286
  116.7 5.3 %collective-permute-start.21 = (bf16[16,8,384]{2,1,0:T(8,128)(2,1)S(1)}, bf16[16,8,384]{2,1,0:T(8,128)(2,1)S(1)}, u32[]{:S(2)}, u32[]{:S(2)}) collective-permute-start(bf16[16,8,384]{2,1,0:T(8,128)(2,1)S(1)} %get-tuple-element.26), channel_id=1, source_target_pairs={{0,3},{1,0},{2,1},{3,2},{4,7},{5,4},{6,5},{7,6},{8,11},{9,8},{10,9... | collective-permute-start | bytes 294920 | tf_op jit(solution)/shard_map/ppermute | solution.py:286
  133.5 4.7 %collective-permute-start.24 = (bf16[16,8,384]{2,1,0:T(8,128)(2,1)S(1)}, bf16[16,8,384]{2,1,0:T(8,128)(2,1)S(1)}, u32[]{:S(2)}, u32[]{:S(2)}) collective-permute-start(bf16[16,8,384]{2,1,0:T(8,128)(2,1)S(1)} %all_to_all.11.refs_0_), channel_id=1, source_target_pairs={{0,3},{1,0},{2,1},{3,2},{4,7},{5,4},{6,5},{7,6},{8,11},{9,8},{10,9... | collective-permute-start | bytes 294920 | tf_op jit(solution)/shard_map/ppermute | solution.py:286
  135.5 5.6 %collective-permute-start.23 = (bf16[16,8,384]{2,1,0:T(8,128)(2,1)S(1)}, bf16[16,8,384]{2,1,0:T(8,128)(2,1)S(1)}, u32[]{:S(2)}, u32[]{:S(2)}) collective-permute-start(bf16[16,8,384]{2,1,0:T(8,128)(2,1)S(1)} %all_to_all.11.refs_0_), channel_id=1, source_target_pairs={{0,2},{1,3},{2,0},{3,1},{4,6},{5,7},{6,4},{7,5},{8,10},{9,11},{10,... | collective-permute-start | bytes 294920 | tf_op jit(solution)/shard_map/ppermute | solution.py:286
  136.2 7.6 %collective-permute-start.22 = (bf16[16,8,384]{2,1,0:T(8,128)(2,1)S(1)}, bf16[16,8,384]{2,1,0:T(8,128)(2,1)S(1)}, u32[]{:S(2)}, u32[]{:S(2)}) collective-permute-start(bf16[16,8,384]{2,1,0:T(8,128)(2,1)S(1)} %all_to_all.11.refs_0_), channel_id=1, source_target_pairs={{0,1},{1,2},{2,3},{3,0},{4,5},{5,6},{6,7},{7,4},{8,9},{9,10},{10,1... | collective-permute-start | bytes 294920 | tf_op jit(solution)/shard_map/ppermute | solution.py:286
where the time goes:
time: 145 us
  waiting for transfers between devices  61.9 us (43%)
  starting transfers between devices  36.8 us (25%)
  blocking collectives  27 us (19%)
  Pallas kernels  12.7 us (9%)
  local copies, waits for them, and re-layouts  4.65 us (3%)
  between operations  2.03 us (1%)
    ppermute x13, waiting for transfers between devices, around(): lax.ppermute(value, axis, [(i, (i + step) % size) for i in range(size)])  31.7 us
    ppermute x11, waiting for transfers between devices, send(): return lax.ppermute(value, axes, pairs)  30.2 us
    ppermute x13, starting transfers between devices, around(): lax.ppermute(value, axis, [(i, (i + step) % size) for i in range(size)])  20.1 us
    all_to_all x1, blocking collectives, backward(): gathered = lax.all_to_all(late, 'seq', 0, 0, tiled=True)  15.5 us
    ppermute x11, starting transfers between devices, send(): return lax.ppermute(value, axes, pairs)  12.5 us
    all_to_all x1, blocking collectives, backward(): share = lax.all_to_all(share, 'seq', 0, 0, tiled=True)  11.4 us
    pallas_call x5, Pallas kernels, small(): pl.pallas_call(kernel, out_shape=tuple((jax.ShapeDtypeStruct(o, BF16) for...  5.46 us
    unnamed x8, local copies, waits for them, and re-layouts  4.65 us
  transfers between devices with their start and end apart: 25, of which 19 were waited for; matrix products, arithmetic and copies ran while one was open for 0% of the time, Pallas kernels for 4%

commit v1 on v0

--- a/solution.py
+++ b/solution.py
@@ -13,6 +13,7 @@
 ANY = pl.BlockSpec(memory_space=pl.ANY)
 SMEM = pl.BlockSpec(memory_space=pltpu.SMEM)
 VMEM = pl.BlockSpec(memory_space=pltpu.VMEM)
+HBM = pl.BlockSpec(memory_space=pltpu.HBM)
 
 ROWS, COLS, CH = 16, 8, 512
 CELLS = ROWS * COLS
@@ -48,22 +49,34 @@
     return jnp.concatenate([v[COLS:], zero], axis=0)
 
 
-def forward_kernel(x_ref, wt_ref, ws_ref, mine_ref, slope_ref, wtt_ref, wst_ref):
+def forward_kernel(
+    x_hbm, wt_hbm, ws_hbm, mine_ref, slope_ref, wtt_ref, wst_ref, x_ref, wt, ws, sems
+):
+    fetch = pltpu.make_async_copy(x_hbm, x_ref, sems.at[TAPS])
+    fetch.start()
+    copies = [pltpu.make_async_copy(ws_hbm.at[k], ws.at[k], sems.at[k]) for k in range(9)]
+    copies += [pltpu.make_async_copy(wt_hbm.at[k], wt.at[k], sems.at[9 + k]) for k in range(3)]
+    for c in copies:
+        c.start()
+    fetch.wait()
     x = x_ref[...].astype(F32)
     cols = column_shifts(x)
+    mine_ref[0] = x.T.astype(BF16)
     pre = None
     for r in range(3):
         for q in range(3):
-            term = nn(row_shift(cols[q - 1], r - 1).astype(BF16), ws_ref[3 * r + q])
+            k = 3 * r + q
+            lhs = row_shift(cols[q - 1], r - 1).astype(BF16)
+            copies[k].wait()
+            term = nn(lhs, ws[k])
             pre = term if pre is None else pre + term
+            wst_ref[k] = ws[k].T
     s = jax.nn.sigmoid(pre)
     slope_ref[...] = s * (1.0 + pre * (1.0 - s))
-    mine_ref[0] = x.T.astype(BF16)
     mine_ref[1] = (pre * s).astype(BF16).astype(F32).T.astype(BF16)
     for k in range(3):
-        wtt_ref[k] = wt_ref[k].T
-    for k in range(9):
-        wst_ref[k] = ws_ref[k].T
+        copies[9 + k].wait()
+        wtt_ref[k] = wt[k].T
 
 
 def forward(x, wt, ws):
@@ -76,11 +89,17 @@
             jax.ShapeDtypeStruct((3, CH, CH), BF16),
             jax.ShapeDtypeStruct((9, CH, CH), BF16),
         ),
-        in_specs=[VMEM] * 3,
+        in_specs=[HBM] * 3,
         out_specs=(VMEM,) * 4,
+        scratch_shapes=[
+            pltpu.VMEM((CELLS, CH), BF16),
+            pltpu.VMEM((3, CH, CH), BF16),
+            pltpu.VMEM((9, CH, CH), BF16),
+            pltpu.SemaphoreType.DMA((TAPS + 1,)),
+        ],
         compiler_params=pltpu.CompilerParams(vmem_limit_bytes=24 << 20),
         cost_estimate=pl.CostEstimate(flops=1208000000, bytes_accessed=13000000, transcendentals=65536),
-    )(x, wt, ws)
+    )(*(pltpu.with_memory_space_constraint(v, pltpu.HBM) for v in (x, wt, ws)))
 
 
 def cotangents(count, refs):
@@ -173,21 +192,15 @@
     ring = refs[:8]
     swapped = refs[8]
     outs = refs[9:13]
-    x, act, left, result, sems = refs[13:]
+    left, result = refs[13:]
     seq, d = lax.axis_index("seq"), lax.axis_index("dp")
     z, core = seq // 2, seq % 2
     half = FRAMES // 2
-    copies = []
+    frame = []
     for k in range(half):
         chip = lax.rem(z + k, half)
-        for which, source in ((core, ring[k]), (1 - core, swapped.at[k])):
-            t = pl.multiple_of((2 * chip + which) * CELLS, CELLS)
-            for part, target in ((0, x), (1, act)):
-                n = len(copies)
-                c = pltpu.make_async_copy(source.at[part], target.at[:, pl.ds(t, CELLS)], sems.at[n])
-                c.start()
-                copies.append(c)
-    g = late_ref[:, :SLICE].astype(F32).reshape(FRAMES * SLICE, CELLS)
+        frame += [2 * chip + core, 2 * chip + 1 - core]
+    g = jnp.stack([late_ref[t, :SLICE] for t in frame]).astype(F32).reshape(FRAMES * SLICE, CELLS)
     lane = lax.broadcasted_iota(jnp.int32, g.shape, 1)
     row, col = lane // COLS, lane % COLS
     for r in range(3):
@@ -208,15 +221,20 @@
     for k in range(3):
         base = (9 + k) * SLICE
         for f in range(FRAMES):
-            if f + k < FRAMES:
-                v = late_ref[f + k, SLICE:]
-            else:
-                v = jnp.zeros((SLICE, CELLS), BF16)
+            t = frame[f] + k
+            v = late_ref[jnp.minimum(t, FRAMES - 1), SLICE:]
+            if k:
+                v = jnp.where(t < FRAMES, v, jnp.zeros((SLICE, CELLS), BF16))
             left[base : base + SLICE, f * CELLS : (f + 1) * CELLS] = v
-    for c in copies:
-        c.wait()
-    spatial = nt(x[...], left[: 9 * SLICE])
-    temporal = nt(act[...], left[9 * SLICE :])
+    spatial = temporal = None
+    for k in range(half):
+        here = slice(2 * k * CELLS, 2 * (k + 1) * CELLS)
+        x = jnp.concatenate([ring[k][0], swapped[k, 0]], axis=1)
+        act = jnp.concatenate([ring[k][1], swapped[k, 1]], axis=1)
+        more = nt(x, left[: 9 * SLICE, here])
+        spatial = more if spatial is None else spatial + more
+        more = nt(act, left[9 * SLICE :, here])
+        temporal = more if temporal is None else temporal + more
     result[:, :, :, : 9 * SLICE] = spatial.reshape(FRAMES, CLIPS, SUB, 9 * SLICE)
     result[:, :, :, 9 * SLICE :] = temporal.reshape(FRAMES, CLIPS, SUB, 3 * SLICE)
     for k in range(CLIPS):
@@ -228,14 +246,11 @@
         weights_kernel,
         name="weight_grads",
         out_shape=(jax.ShapeDtypeStruct((FRAMES, SUB, WIDE), BF16),) * CLIPS,
-        in_specs=[VMEM] + [ANY] * 9,
+        in_specs=[VMEM] * 10,
         out_specs=(VMEM,) * CLIPS,
         scratch_shapes=[
-            pltpu.VMEM((CH, FRAMES * CELLS), BF16),
-            pltpu.VMEM((CH, FRAMES * CELLS), BF16),
             pltpu.VMEM((WIDE, FRAMES * CELLS), BF16),
             pltpu.VMEM((FRAMES, CLIPS, SUB, WIDE), F32),
-            pltpu.SemaphoreType.DMA((4 * FRAMES // 2,)),
         ],
         compiler_params=pltpu.CompilerParams(vmem_limit_bytes=24 << 20),
         cost_estimate=pl.CostEstimate(flops=1610000000, bytes_accessed=5000000, transcendentals=0),
@@ -299,6 +314,7 @@
     ahead2 = send(cot, axes, sizes, (0, -2))
     ahead1 = send(cot, axes, sizes, (0, -1))
     mine, slope, wtt, wst = forward(x, wt, ws)
+    frame_start, frame_count, slope = lax.optimization_barrier((frame_start, frame_count, slope))
     head = [frame_start, frame_count, cot, ahead1, ahead2]
     head_specs = [SMEM, SMEM] + [VMEM] * 3
     ring = {0: mine}

time: 145 us -> 141 us (0.972)
  local copies, waits for them, and re-layouts: 4.65 us -> 0.01 us
    unnamed x8 -> x2, local copies, waits for them, and re-layouts: 4.65 us -> 0.01 us
    pallas_call x1, Pallas kernels: 1.86 us -> 3.87 us  [forward(): pl.pallas_call(forward_kernel, name='block_forward', out_shape=(jax.Shape...]
    pallas_call x1, Pallas kernels: 3.91 us -> 2.19 us  [weights(): pl.pallas_call(weights_kernel, name='weight_grads', out_shape=(jax.ShapeD...]
where the time goes in v1:
time: 141 us
  waiting for transfers between devices  61.9 us (44%)
  starting transfers between devices  36.7 us (26%)
  blocking collectives  26.9 us (19%)
  Pallas kernels  13 us (9%)
  between operations  2.02 us (1%)
    ppermute x13, waiting for transfers between devices, around(): lax.ppermute(value, axis, [(i, (i + step) % size) for i in range(size)])  31.7 us
    ppermute x11, waiting for transfers between devices, send(): return lax.ppermute(value, axes, pairs)  30.2 us
    ppermute x13, starting transfers between devices, around(): lax.ppermute(value, axis, [(i, (i + step) % size) for i in range(size)])  20 us
    all_to_all x1, blocking collectives, backward(): gathered = lax.all_to_all(late, 'seq', 0, 0, tiled=True)  15.5 us
    ppermute x11, starting transfers between devices, send(): return lax.ppermute(value, axes, pairs)  12.5 us
    all_to_all x1, blocking collectives, backward(): share = lax.all_to_all(share, 'seq', 0, 0, tiled=True)  11.4 us
    pallas_call x5, Pallas kernels, small(): pl.pallas_call(kernel, out_shape=tuple((jax.ShapeDtypeStruct(o, BF16) for...  5.47 us
    ppermute x1, starting transfers between devices, backward(): swapped = lax.ppermute(packed, 'seq', [(i, i ^ 1) for i in range(FRAMES)])  4.2 us
  transfers between devices with their start and end apart: 25, of which 19 were waited for; matrix products, arithmetic and copies ran while one was open for 0% of the time, Pallas kernels for 4%

profile of v1, /device:TPU:1, one launch (start us, length us, event | category | flops | bytes accessed | tf_op | source)
XLA Modules:
  0.0 140.6 jit_solution(14571303582553922379)
XLA Ops:
  0.6 3.9 %block_forward.1 = (bf16[2,512,128]{2,1,0:T(8,128)(2,1)S(1)}, f32[128,512]{1,0:T(8,128)S(1)}, bf16[3,512,512]{2,1,0:T(8,128)(2,1)S(1)}, bf16[9,512,512]{2,1,0:T(8,128)(2,1)S(1)}) custom-call(bf16[128,512]{1,0:T(8,128)(2,1)} %bitcast.15, bf16[3,512,512]{2,1,0:T(8,128)(2,1)} %bitcast.14, bf16[9,512,512]{2,1,0:T(8,128)(2,1)} %bitcast.13), custom_call_target="tpu_custom_call" | custom-call | flops 1208000000 | bytes 13000000 | tf_op jit(solution)/shard_map/block_forward/pallas_call | solution.py:83
  4.5 2.5 %collective-permute-start.14 = (bf16[2,512,128]{2,1,0:T(8,128)(2,1)S(1)}, bf16[2,512,128]{2,1,0:T(8,128)(2,1)S(1)}, u32[]{:S(2)}, u32[]{:S(2)}) collective-permute-start(bf16[2,512,128]{2,1,0:T(8,128)(2,1)S(1)} %get-tuple-element.28.refs_0_), channel_id=1, source_target_pairs={{0,8},{4,12},{8,16},{12,20},{16,24},{20,28},{24,32},{28,36},{32,40... | collective-permute-start | bytes 786440 | tf_op jit(solution)/shard_map/ppermute | solution.py:301
  7.1 4.0 %collective-permute-start.11 = (bf16[2,512,128]{2,1,0:T(8,128)(2,1)S(1)}, bf16[2,512,128]{2,1,0:T(8,128)(2,1)S(1)}, u32[]{:S(2)}, u32[]{:S(2)}) collective-permute-start(bf16[2,512,128]{2,1,0:T(8,128)(2,1)S(1)} %get-tuple-element.28.refs_0_), channel_id=1, source_target_pairs={{0,56},{4,60},{8,0},{12,4},{16,8},{20,12},{24,16},{28,20},{32,24},... | collective-permute-start | bytes 786440 | tf_op jit(solution)/shard_map/ppermute | solution.py:301
  11.1 5.9 %collective-permute-done.14.refs_7_ = bf16[2,512,128]{2,1,0:T(8,128)(2,1)S(1)} collective-permute-done((bf16[2,512,128]{2,1,0:T(8,128)(2,1)S(1)}, bf16[2,512,128]{2,1,0:T(8,128)(2,1)S(1)}, u32[]{:S(2)}, u32[]{:S(2)}) %collective-permute-start.14) | collective-permute-done | bytes 262176 | tf_op jit(solution)/shard_map/ppermute | solution.py:301
  17.0 2.7 %collective-permute-start.12 = (bf16[2,512,128]{2,1,0:T(8,128)(2,1)S(1)}, bf16[2,512,128]{2,1,0:T(8,128)(2,1)S(1)}, u32[]{:S(2)}, u32[]{:S(2)}) collective-permute-start(bf16[2,512,128]{2,1,0:T(8,128)(2,1)S(1)} %collective-permute-done.11.refs_1_), channel_id=1, source_target_pairs={{0,56},{4,60},{8,0},{12,4},{16,8},{20,12},{24,16},{28,20},{32,24},... | collective-permute-start | bytes 786440 | tf_op jit(solution)/shard_map/ppermute | solution.py:301
  19.7 5.1 %collective-permute-done.15.refs_6_ = bf16[2,512,128]{2,1,0:T(8,128)(2,1)S(1)} collective-permute-done((bf16[2,512,128]{2,1,0:T(8,128)(2,1)S(1)}, bf16[2,512,128]{2,1,0:T(8,128)(2,1)S(1)}, u32[]{:S(2)}, u32[]{:S(2)}) %collective-permute-start.15) | collective-permute-done | bytes 262176 | tf_op jit(solution)/shard_map/ppermute | solution.py:301
  24.8 2.7 %collective-permute-start.13 = (bf16[2,512,128]{2,1,0:T(8,128)(2,1)S(1)}, bf16[2,512,128]{2,1,0:T(8,128)(2,1)S(1)}, u32[]{:S(2)}, u32[]{:S(2)}) collective-permute-start(bf16[2,512,128]{2,1,0:T(8,128)(2,1)S(1)} %collective-permute-done.12.refs_2_), channel_id=1, source_target_pairs={{0,56},{4,60},{8,0},{12,4},{16,8},{20,12},{24,16},{28,20},{32,24},... | collective-permute-start | bytes 786440 | tf_op jit(solution)/shard_map/ppermute | solution.py:301
  27.5 4.3 %collective-permute-done.16.refs_5_ = bf16[2,512,128]{2,1,0:T(8,128)(2,1)S(1)} collective-permute-done((bf16[2,512,128]{2,1,0:T(8,128)(2,1)S(1)}, bf16[2,512,128]{2,1,0:T(8,128)(2,1)S(1)}, u32[]{:S(2)}, u32[]{:S(2)}) %collective-permute-start.16) | collective-permute-done | bytes 262176 | tf_op jit(solution)/shard_map/ppermute | solution.py:301
  31.8 6.4 %collective-permute-done.17.refs_4_ = bf16[2,512,128]{2,1,0:T(8,128)(2,1)S(1)} collective-permute-done((bf16[2,512,128]{2,1,0:T(8,128)(2,1)S(1)}, bf16[2,512,128]{2,1,0:T(8,128)(2,1)S(1)}, u32[]{:S(2)}, u32[]{:S(2)}) %collective-permute-start.17) | collective-permute-done | bytes 262176 | tf_op jit(solution)/shard_map/ppermute | solution.py:301
  38.5 4.2 %collective-permute-start.18 = (bf16[8,2,512,128]{3,2,1,0:T(8,128)(2,1)S(1)}, bf16[8,2,512,128]{3,2,1,0:T(8,128)(2,1)S(1)}, u32[]{:S(2)}, u32[]{:S(2)}) collective-permute-start(bf16[8,2,512,128]{3,2,1,0:T(8,128)(2,1)S(1)} %pack.1), channel_id=1, source_target_pairs={{0,4},{4,0},{8,12},{12,8},{16,20},{20,16},{24,28},{28,24},{32,36},... | collective-permute-start | bytes 6291464 | tf_op jit(solution)/shard_map/ppermute | solution.py:352
  44.1 3.5 %collective-permute-done.1.refs_4_ = bf16[128,512]{1,0:T(8,128)(2,1)S(1)} collective-permute-done((bf16[128,512]{1,0:T(8,128)(2,1)S(1)}, bf16[128,512]{1,0:T(8,128)(2,1)S(1)}, u32[]{:S(2)}, u32[]{:S(2)}) %collective-permute-start.1) | collective-permute-done | bytes 131104 | tf_op jit(solution)/shard_map/ppermute | solution.py:297
  47.6 1.7 %collective-permute-done.refs_3_ = bf16[128,512]{1,0:T(8,128)(2,1)S(1)} collective-permute-done((bf16[128,512]{1,0:T(8,128)(2,1)S(1)}, bf16[128,512]{1,0:T(8,128)(2,1)S(1)}, u32[]{:S(2)}, u32[]{:S(2)}) %collective-permute-start) | collective-permute-done | bytes 131104 | tf_op jit(solution)/shard_map/ppermute | solution.py:297
  50.5 3.7 %collective-permute-start.4 = (bf16[128,512]{1,0:T(8,128)(2,1)S(1)}, bf16[128,512]{1,0:T(8,128)(2,1)S(1)}, u32[]{:S(2)}, u32[]{:S(2)}) collective-permute-start(bf16[128,512]{1,0:T(8,128)(2,1)S(1)} %shard_map.85), channel_id=1, source_target_pairs={{0,248},{4,252},{8,192},{12,196},{16,200},{20,204},{24,208},{28,21... | collective-permute-start | bytes 393224 | tf_op jit(solution)/shard_map/ppermute | solution.py:297
  54.7 2.9 %collective-permute-done.4.refs_7_ = bf16[128,512]{1,0:T(8,128)(2,1)S(1)} collective-permute-done((bf16[128,512]{1,0:T(8,128)(2,1)S(1)}, bf16[128,512]{1,0:T(8,128)(2,1)S(1)}, u32[]{:S(2)}, u32[]{:S(2)}) %collective-permute-start.4) | collective-permute-done | bytes 131104 | tf_op jit(solution)/shard_map/ppermute | solution.py:297
  57.6 3.8 %collective-permute-done.3.refs_6_ = bf16[128,512]{1,0:T(8,128)(2,1)S(1)} collective-permute-done((bf16[128,512]{1,0:T(8,128)(2,1)S(1)}, bf16[128,512]{1,0:T(8,128)(2,1)S(1)}, u32[]{:S(2)}, u32[]{:S(2)}) %collective-permute-start.3) | collective-permute-done | bytes 131104 | tf_op jit(solution)/shard_map/ppermute | solution.py:297
  61.4 1.5 %collective-permute-done.2.refs_5_ = bf16[128,512]{1,0:T(8,128)(2,1)S(1)} collective-permute-done((bf16[128,512]{1,0:T(8,128)(2,1)S(1)}, bf16[128,512]{1,0:T(8,128)(2,1)S(1)}, u32[]{:S(2)}, u32[]{:S(2)}) %collective-permute-start.2) | collective-permute-done | bytes 131104 | tf_op jit(solution)/shard_map/ppermute | solution.py:297
  64.1 2.9 %collective-permute-start.7 = (bf16[128,512]{1,0:T(8,128)(2,1)S(1)}, bf16[128,512]{1,0:T(8,128)(2,1)S(1)}, u32[]{:S(2)}, u32[]{:S(2)}) collective-permute-start(bf16[128,512]{1,0:T(8,128)(2,1)S(1)} %shard_map.86), channel_id=1, source_target_pairs={{0,248},{4,252},{8,192},{12,196},{16,200},{20,204},{24,208},{28,21... | collective-permute-start | bytes 393224 | tf_op jit(solution)/shard_map/ppermute | solution.py:297
  68.3 2.2 %collective-permute-done.7.refs_7_ = bf16[128,512]{1,0:T(8,128)(2,1)S(1)} collective-permute-done((bf16[128,512]{1,0:T(8,128)(2,1)S(1)}, bf16[128,512]{1,0:T(8,128)(2,1)S(1)}, u32[]{:S(2)}, u32[]{:S(2)}) %collective-permute-start.7) | collective-permute-done | bytes 131104 | tf_op jit(solution)/shard_map/ppermute | solution.py:297
  70.5 3.3 %collective-permute-done.6.refs_6_ = bf16[128,512]{1,0:T(8,128)(2,1)S(1)} collective-permute-done((bf16[128,512]{1,0:T(8,128)(2,1)S(1)}, bf16[128,512]{1,0:T(8,128)(2,1)S(1)}, u32[]{:S(2)}, u32[]{:S(2)}) %collective-permute-start.6) | collective-permute-done | bytes 131104 | tf_op jit(solution)/shard_map/ppermute | solution.py:297
  73.8 2.4 %collective-permute-done.5.refs_5_ = bf16[128,512]{1,0:T(8,128)(2,1)S(1)} collective-permute-done((bf16[128,512]{1,0:T(8,128)(2,1)S(1)}, bf16[128,512]{1,0:T(8,128)(2,1)S(1)}, u32[]{:S(2)}, u32[]{:S(2)}) %collective-permute-start.5) | collective-permute-done | bytes 131104 | tf_op jit(solution)/shard_map/ppermute | solution.py:297
  77.4 3.9 %collective-permute-start.10 = (bf16[128,512]{1,0:T(8,128)(2,1)S(1)}, bf16[128,512]{1,0:T(8,128)(2,1)S(1)}, u32[]{:S(2)}, u32[]{:S(2)}) collective-permute-start(bf16[128,512]{1,0:T(8,128)(2,1)S(1)} %shard_map.87), channel_id=1, source_target_pairs={{0,248},{4,252},{8,192},{12,196},{16,200},{20,204},{24,208},{28,21... | collective-permute-start | bytes 393224 | tf_op jit(solution)/shard_map/ppermute | solution.py:297
  81.4 2.4 %collective-permute-done.10.refs_7_ = bf16[128,512]{1,0:T(8,128)(2,1)S(1)} collective-permute-done((bf16[128,512]{1,0:T(8,128)(2,1)S(1)}, bf16[128,512]{1,0:T(8,128)(2,1)S(1)}, u32[]{:S(2)}, u32[]{:S(2)}) %collective-permute-start.10) | collective-permute-done | bytes 131104 | tf_op jit(solution)/shard_map/ppermute | solution.py:297
  83.8 4.8 %collective-permute-done.9.refs_6_ = bf16[128,512]{1,0:T(8,128)(2,1)S(1)} collective-permute-done((bf16[128,512]{1,0:T(8,128)(2,1)S(1)}, bf16[128,512]{1,0:T(8,128)(2,1)S(1)}, u32[]{:S(2)}, u32[]{:S(2)}) %collective-permute-start.9) | collective-permute-done | bytes 131104 | tf_op jit(solution)/shard_map/ppermute | solution.py:297
  88.6 1.7 %collective-permute-done.8.refs_5_ = bf16[128,512]{1,0:T(8,128)(2,1)S(1)} collective-permute-done((bf16[128,512]{1,0:T(8,128)(2,1)S(1)}, bf16[128,512]{1,0:T(8,128)(2,1)S(1)}, u32[]{:S(2)}, u32[]{:S(2)}) %collective-permute-start.8) | collective-permute-done | bytes 131104 | tf_op jit(solution)/shard_map/ppermute | solution.py:297
  90.8 15.5 %all_to_all.10.late_ref = bf16[16,64,128]{2,1,0:T(8,128)(2,1)S(1)} all-to-all(bf16[16,64,128]{2,1,0:T(8,128)(2,1)S(1)} %get-tuple-element.27), channel_id=1, replica_groups=mesh['pipe'=4,'seq'=16,'dp'=4] {'seq'}, dimensions={0} | all-to-all | bytes 524288 | tf_op jit(solution)/shard_map/all_to_all | solution.py:349
  106.3 2.2 %weight_grads.1 = (bf16[16,8,384]{2,1,0:T(8,128)(2,1)S(1)}, bf16[16,8,384]{2,1,0:T(8,128)(2,1)S(1)}, bf16[16,8,384]{2,1,0:T(8,128)(2,1)S(1)}, bf16[16,8,384]{2,1,0:T(8,128)(2,1)S(1)}) custom-call(bf16[16,64,128]{2,1,0:T(8,128)(2,1)S(1)} %all_to_all.10.late_ref, bf16[2,512,128]{2,1,0:T(8,128)(2,1)S(1)} %get-tuple-element.28.refs_0_, ...), custom_call_target="tpu_custom_call" | custom-call | flops 1610000000 | bytes 5000000 | tf_op jit(solution)/shard_map/weight_grads/pallas_call | solution.py:245
  109.8 2.5 %collective-permute-start.20 = (bf16[16,8,384]{2,1,0:T(8,128)(2,1)S(1)}, bf16[16,8,384]{2,1,0:T(8,128)(2,1)S(1)}, u32[]{:S(2)}, u32[]{:S(2)}) collective-permute-start(bf16[16,8,384]{2,1,0:T(8,128)(2,1)S(1)} %get-tuple-element.31), channel_id=1, source_target_pairs={{0,2},{1,3},{2,0},{3,1},{4,6},{5,7},{6,4},{7,5},{8,10},{9,11},{10,... | collective-permute-start | bytes 294920 | tf_op jit(solution)/shard_map/ppermute | solution.py:301
  114.5 3.1 %collective-permute-done.20 = bf16[16,8,384]{2,1,0:T(8,128)(2,1)S(1)} collective-permute-done((bf16[16,8,384]{2,1,0:T(8,128)(2,1)S(1)}, bf16[16,8,384]{2,1,0:T(8,128)(2,1)S(1)}, u32[]{:S(2)}, u32[]{:S(2)}) %collective-permute-start.20) | collective-permute-done | bytes 98336 | tf_op jit(solution)/shard_map/ppermute | solution.py:301
  117.7 11.4 %all_to_all.11.refs_0_ = bf16[16,8,384]{2,1,0:T(8,128)(2,1)S(1)} all-to-all(bf16[16,8,384]{2,1,0:T(8,128)(2,1)S(1)} %add_convert_fusion), channel_id=1, replica_groups=mesh['pipe'=4,'seq'=16,'dp'=4] {'seq'}, dimensions={0} | all-to-all | bytes 196608 | tf_op jit(solution)/shard_map/all_to_all | solution.py:359
  129.1 2.0 %collective-permute-start.24 = (bf16[16,8,384]{2,1,0:T(8,128)(2,1)S(1)}, bf16[16,8,384]{2,1,0:T(8,128)(2,1)S(1)}, u32[]{:S(2)}, u32[]{:S(2)}) collective-permute-start(bf16[16,8,384]{2,1,0:T(8,128)(2,1)S(1)} %all_to_all.11.refs_0_), channel_id=1, source_target_pairs={{0,3},{1,0},{2,1},{3,2},{4,7},{5,4},{6,5},{7,6},{8,11},{9,8},{10,9... | collective-permute-start | bytes 294920 | tf_op jit(solution)/shard_map/ppermute | solution.py:301
  133.7 3.0 %collective-permute-done.23.refs_2_ = bf16[16,8,384]{2,1,0:T(8,128)(2,1)S(1)} collective-permute-done((bf16[16,8,384]{2,1,0:T(8,128)(2,1)S(1)}, bf16[16,8,384]{2,1,0:T(8,128)(2,1)S(1)}, u32[]{:S(2)}, u32[]{:S(2)}) %collective-permute-start.23) | collective-permute-done | bytes 98336 | tf_op jit(solution)/shard_map/ppermute | solution.py:301
  136.7 2.7 %collective-permute-done.22.refs_1_ = bf16[16,8,384]{2,1,0:T(8,128)(2,1)S(1)} collective-permute-done((bf16[16,8,384]{2,1,0:T(8,128)(2,1)S(1)}, bf16[16,8,384]{2,1,0:T(8,128)(2,1)S(1)}, u32[]{:S(2)}, u32[]{:S(2)}) %collective-permute-start.22) | collective-permute-done | bytes 98336 | tf_op jit(solution)/shard_map/ppermute | solution.py:301
  (32 shorter events, 13.7 us)
Async XLA Ops:
  4.5 38.2 %copy-start = (bf16[1,1,16,8,512]{4,3,2,1,0:T(8,128)(2,1)S(1)}, bf16[1,1,16,8,512]{4,3,2,1,0:T(8,128)(2,1)}, u32[]{:S(2)}) copy-start(bf16[1,1,16,8,512]{4,3,2,1,0:T(8,128)(2,1)} %param.9) | copy-start | bytes 393220
  4.5 12.5 %collective-permute-start.14 = (bf16[2,512,128]{2,1,0:T(8,128)(2,1)S(1)}, bf16[2,512,128]{2,1,0:T(8,128)(2,1)S(1)}, u32[]{:S(2)}, u32[]{:S(2)}) collective-permute-start(bf16[2,512,128]{2,1,0:T(8,128)(2,1)S(1)} %get-tuple-element.28.refs_0_), channel_id=1, source_target_pairs={{0,8},{4,12},{8,16},{12,20},{16,24},{20,28},{24,32},{28,36},{32,40... | collective-permute-start | bytes 786440 | tf_op jit(solution)/shard_map/ppermute | solution.py:301
  7.1 10.0 %collective-permute-start.11 = (bf16[2,512,128]{2,1,0:T(8,128)(2,1)S(1)}, bf16[2,512,128]{2,1,0:T(8,128)(2,1)S(1)}, u32[]{:S(2)}, u32[]{:S(2)}) collective-permute-start(bf16[2,512,128]{2,1,0:T(8,128)(2,1)S(1)} %get-tuple-element.28.refs_0_), channel_id=1, source_target_pairs={{0,56},{4,60},{8,0},{12,4},{16,8},{20,12},{24,16},{28,20},{32,24},... | collective-permute-start | bytes 786440 | tf_op jit(solution)/shard_map/ppermute | solution.py:301
  17.0 7.8 %collective-permute-start.15 = (bf16[2,512,128]{2,1,0:T(8,128)(2,1)S(1)}, bf16[2,512,128]{2,1,0:T(8,128)(2,1)S(1)}, u32[]{:S(2)}, u32[]{:S(2)}) collective-permute-start(bf16[2,512,128]{2,1,0:T(8,128)(2,1)S(1)} %collective-permute-done.14.refs_7_), channel_id=1, source_target_pairs={{0,8},{4,12},{8,16},{12,20},{16,24},{20,28},{24,32},{28,36},{32,40... | collective-permute-start | bytes 786440 | tf_op jit(solution)/shard_map/ppermute | solution.py:301
  17.0 7.8 %collective-permute-start.12 = (bf16[2,512,128]{2,1,0:T(8,128)(2,1)S(1)}, bf16[2,512,128]{2,1,0:T(8,128)(2,1)S(1)}, u32[]{:S(2)}, u32[]{:S(2)}) collective-permute-start(bf16[2,512,128]{2,1,0:T(8,128)(2,1)S(1)} %collective-permute-done.11.refs_1_), channel_id=1, source_target_pairs={{0,56},{4,60},{8,0},{12,4},{16,8},{20,12},{24,16},{28,20},{32,24},... | collective-permute-start | bytes 786440 | tf_op jit(solution)/shard_map/ppermute | solution.py:301
  24.8 7.0 %collective-permute-start.16 = (bf16[2,512,128]{2,1,0:T(8,128)(2,1)S(1)}, bf16[2,512,128]{2,1,0:T(8,128)(2,1)S(1)}, u32[]{:S(2)}, u32[]{:S(2)}) collective-permute-start(bf16[2,512,128]{2,1,0:T(8,128)(2,1)S(1)} %collective-permute-done.15.refs_6_), channel_id=1, source_target_pairs={{0,8},{4,12},{8,16},{12,20},{16,24},{20,28},{24,32},{28,36},{32,40... | collective-permute-start | bytes 786440 | tf_op jit(solution)/shard_map/ppermute | solution.py:301
  24.8 7.0 %collective-permute-start.13 = (bf16[2,512,128]{2,1,0:T(8,128)(2,1)S(1)}, bf16[2,512,128]{2,1,0:T(8,128)(2,1)S(1)}, u32[]{:S(2)}, u32[]{:S(2)}) collective-permute-start(bf16[2,512,128]{2,1,0:T(8,128)(2,1)S(1)} %collective-permute-done.12.refs_2_), channel_id=1, source_target_pairs={{0,56},{4,60},{8,0},{12,4},{16,8},{20,12},{24,16},{28,20},{32,24},... | collective-permute-start | bytes 786440 | tf_op jit(solution)/shard_map/ppermute | solution.py:301
  31.8 6.4 %collective-permute-start.17 = (bf16[2,512,128]{2,1,0:T(8,128)(2,1)S(1)}, bf16[2,512,128]{2,1,0:T(8,128)(2,1)S(1)}, u32[]{:S(2)}, u32[]{:S(2)}) collective-permute-start(bf16[2,512,128]{2,1,0:T(8,128)(2,1)S(1)} %collective-permute-done.16.refs_5_), channel_id=1, source_target_pairs={{0,8},{4,12},{8,16},{12,20},{16,24},{20,28},{24,32},{28,36},{32,40... | collective-permute-start | bytes 786440 | tf_op jit(solution)/shard_map/ppermute | solution.py:301
  38.5 67.8 %collective-permute-start.18 = (bf16[8,2,512,128]{3,2,1,0:T(8,128)(2,1)S(1)}, bf16[8,2,512,128]{3,2,1,0:T(8,128)(2,1)S(1)}, u32[]{:S(2)}, u32[]{:S(2)}) collective-permute-start(bf16[8,2,512,128]{3,2,1,0:T(8,128)(2,1)S(1)} %pack.1), channel_id=1, source_target_pairs={{0,4},{4,0},{8,12},{12,8},{16,20},{20,16},{24,28},{28,24},{32,36},... | collective-permute-start | bytes 6291464 | tf_op jit(solution)/shard_map/ppermute | solution.py:352
  42.7 5.0 %collective-permute-start.1 = (bf16[128,512]{1,0:T(8,128)(2,1)S(1)}, bf16[128,512]{1,0:T(8,128)(2,1)S(1)}, u32[]{:S(2)}, u32[]{:S(2)}) collective-permute-start(bf16[128,512]{1,0:T(8,128)(2,1)S(1)} %bitcast.7), channel_id=1, source_target_pairs={{0,56},{4,60},{8,0},{12,4},{16,8},{20,12},{24,16},{28,20},{32,24},... | collective-permute-start | bytes 393224 | tf_op jit(solution)/shard_map/ppermute | solution.py:297
  42.7 6.6 %collective-permute-start = (bf16[128,512]{1,0:T(8,128)(2,1)S(1)}, bf16[128,512]{1,0:T(8,128)(2,1)S(1)}, u32[]{:S(2)}, u32[]{:S(2)}) collective-permute-start(bf16[128,512]{1,0:T(8,128)(2,1)S(1)} %bitcast.8), channel_id=1, source_target_pairs={{0,60},{4,0},{8,4},{12,8},{16,12},{20,16},{24,20},{28,24},{32,28},... | collective-permute-start | bytes 393224 | tf_op jit(solution)/shard_map/ppermute | solution.py:297
  50.5 7.1 %collective-permute-start.4 = (bf16[128,512]{1,0:T(8,128)(2,1)S(1)}, bf16[128,512]{1,0:T(8,128)(2,1)S(1)}, u32[]{:S(2)}, u32[]{:S(2)}) collective-permute-start(bf16[128,512]{1,0:T(8,128)(2,1)S(1)} %shard_map.85), channel_id=1, source_target_pairs={{0,248},{4,252},{8,192},{12,196},{16,200},{20,204},{24,208},{28,21... | collective-permute-start | bytes 393224 | tf_op jit(solution)/shard_map/ppermute | solution.py:297
  54.2 7.2 %collective-permute-start.3 = (bf16[128,512]{1,0:T(8,128)(2,1)S(1)}, bf16[128,512]{1,0:T(8,128)(2,1)S(1)}, u32[]{:S(2)}, u32[]{:S(2)}) collective-permute-start(bf16[128,512]{1,0:T(8,128)(2,1)S(1)} %shard_map.85), channel_id=1, source_target_pairs={{0,252},{4,192},{8,196},{12,200},{16,204},{20,208},{24,212},{28,21... | collective-permute-start | bytes 393224 | tf_op jit(solution)/shard_map/ppermute | solution.py:297
  54.2 8.7 %collective-permute-start.2 = (bf16[128,512]{1,0:T(8,128)(2,1)S(1)}, bf16[128,512]{1,0:T(8,128)(2,1)S(1)}, u32[]{:S(2)}, u32[]{:S(2)}) collective-permute-start(bf16[128,512]{1,0:T(8,128)(2,1)S(1)} %shard_map.85), channel_id=1, source_target_pairs={{0,192},{4,196},{8,200},{12,204},{16,208},{20,212},{24,216},{28,22... | collective-permute-start | bytes 393224 | tf_op jit(solution)/shard_map/ppermute | solution.py:297
  64.1 6.4 %collective-permute-start.7 = (bf16[128,512]{1,0:T(8,128)(2,1)S(1)}, bf16[128,512]{1,0:T(8,128)(2,1)S(1)}, u32[]{:S(2)}, u32[]{:S(2)}) collective-permute-start(bf16[128,512]{1,0:T(8,128)(2,1)S(1)} %shard_map.86), channel_id=1, source_target_pairs={{0,248},{4,252},{8,192},{12,196},{16,200},{20,204},{24,208},{28,21... | collective-permute-start | bytes 393224 | tf_op jit(solution)/shard_map/ppermute | solution.py:297
  66.9 6.9 %collective-permute-start.6 = (bf16[128,512]{1,0:T(8,128)(2,1)S(1)}, bf16[128,512]{1,0:T(8,128)(2,1)S(1)}, u32[]{:S(2)}, u32[]{:S(2)}) collective-permute-start(bf16[128,512]{1,0:T(8,128)(2,1)S(1)} %shard_map.86), channel_id=1, source_target_pairs={{0,252},{4,192},{8,196},{12,200},{16,204},{20,208},{24,212},{28,21... | collective-permute-start | bytes 393224 | tf_op jit(solution)/shard_map/ppermute | solution.py:297
  67.3 8.9 %collective-permute-start.5 = (bf16[128,512]{1,0:T(8,128)(2,1)S(1)}, bf16[128,512]{1,0:T(8,128)(2,1)S(1)}, u32[]{:S(2)}, u32[]{:S(2)}) collective-permute-start(bf16[128,512]{1,0:T(8,128)(2,1)S(1)} %shard_map.86), channel_id=1, source_target_pairs={{0,192},{4,196},{8,200},{12,204},{16,208},{20,212},{24,216},{28,22... | collective-permute-start | bytes 393224 | tf_op jit(solution)/shard_map/ppermute | solution.py:297
  77.4 6.4 %collective-permute-start.10 = (bf16[128,512]{1,0:T(8,128)(2,1)S(1)}, bf16[128,512]{1,0:T(8,128)(2,1)S(1)}, u32[]{:S(2)}, u32[]{:S(2)}) collective-permute-start(bf16[128,512]{1,0:T(8,128)(2,1)S(1)} %shard_map.87), channel_id=1, source_target_pairs={{0,248},{4,252},{8,192},{12,196},{16,200},{20,204},{24,208},{28,21... | collective-permute-start | bytes 393224 | tf_op jit(solution)/shard_map/ppermute | solution.py:297
  81.3 7.3 %collective-permute-start.9 = (bf16[128,512]{1,0:T(8,128)(2,1)S(1)}, bf16[128,512]{1,0:T(8,128)(2,1)S(1)}, u32[]{:S(2)}, u32[]{:S(2)}) collective-permute-start(bf16[128,512]{1,0:T(8,128)(2,1)S(1)} %shard_map.87), channel_id=1, source_target_pairs={{0,252},{4,192},{8,196},{12,200},{16,204},{20,208},{24,212},{28,21... | collective-permute-start | bytes 393224 | tf_op jit(solution)/shard_map/ppermute | solution.py:297
  81.3 8.9 %collective-permute-start.8 = (bf16[128,512]{1,0:T(8,128)(2,1)S(1)}, bf16[128,512]{1,0:T(8,128)(2,1)S(1)}, u32[]{:S(2)}, u32[]{:S(2)}) collective-permute-start(bf16[128,512]{1,0:T(8,128)(2,1)S(1)} %shard_map.87), channel_id=1, source_target_pairs={{0,192},{4,196},{8,200},{12,204},{16,208},{20,212},{24,216},{28,22... | collective-permute-start | bytes 393224 | tf_op jit(solution)/shard_map/ppermute | solution.py:297
  108.5 6.0 %collective-permute-start.19 = (bf16[16,8,384]{2,1,0:T(8,128)(2,1)S(1)}, bf16[16,8,384]{2,1,0:T(8,128)(2,1)S(1)}, u32[]{:S(2)}, u32[]{:S(2)}) collective-permute-start(bf16[16,8,384]{2,1,0:T(8,128)(2,1)S(1)} %get-tuple-element.30), channel_id=1, source_target_pairs={{0,1},{1,2},{2,3},{3,0},{4,5},{5,6},{6,7},{7,4},{8,9},{9,10},{10,1... | collective-permute-start | bytes 294920 | tf_op jit(solution)/shard_map/ppermute | solution.py:301
  109.8 7.8 %collective-permute-start.20 = (bf16[16,8,384]{2,1,0:T(8,128)(2,1)S(1)}, bf16[16,8,384]{2,1,0:T(8,128)(2,1)S(1)}, u32[]{:S(2)}, u32[]{:S(2)}) collective-permute-start(bf16[16,8,384]{2,1,0:T(8,128)(2,1)S(1)} %get-tuple-element.31), channel_id=1, source_target_pairs={{0,2},{1,3},{2,0},{3,1},{4,6},{5,7},{6,4},{7,5},{8,10},{9,11},{10,... | collective-permute-start | bytes 294920 | tf_op jit(solution)/shard_map/ppermute | solution.py:301
  112.3 5.3 %collective-permute-start.21 = (bf16[16,8,384]{2,1,0:T(8,128)(2,1)S(1)}, bf16[16,8,384]{2,1,0:T(8,128)(2,1)S(1)}, u32[]{:S(2)}, u32[]{:S(2)}) collective-permute-start(bf16[16,8,384]{2,1,0:T(8,128)(2,1)S(1)} %get-tuple-element.32), channel_id=1, source_target_pairs={{0,3},{1,0},{2,1},{3,2},{4,7},{5,4},{6,5},{7,6},{8,11},{9,8},{10,9... | collective-permute-start | bytes 294920 | tf_op jit(solution)/shard_map/ppermute | solution.py:301
  129.1 4.7 %collective-permute-start.24 = (bf16[16,8,384]{2,1,0:T(8,128)(2,1)S(1)}, bf16[16,8,384]{2,1,0:T(8,128)(2,1)S(1)}, u32[]{:S(2)}, u32[]{:S(2)}) collective-permute-start(bf16[16,8,384]{2,1,0:T(8,128)(2,1)S(1)} %all_to_all.11.refs_0_), channel_id=1, source_target_pairs={{0,3},{1,0},{2,1},{3,2},{4,7},{5,4},{6,5},{7,6},{8,11},{9,8},{10,9... | collective-permute-start | bytes 294920 | tf_op jit(solution)/shard_map/ppermute | solution.py:301
  131.1 5.6 %collective-permute-start.23 = (bf16[16,8,384]{2,1,0:T(8,128)(2,1)S(1)}, bf16[16,8,384]{2,1,0:T(8,128)(2,1)S(1)}, u32[]{:S(2)}, u32[]{:S(2)}) collective-permute-start(bf16[16,8,384]{2,1,0:T(8,128)(2,1)S(1)} %all_to_all.11.refs_0_), channel_id=1, source_target_pairs={{0,2},{1,3},{2,0},{3,1},{4,6},{5,7},{6,4},{7,5},{8,10},{9,11},{10,... | collective-permute-start | bytes 294920 | tf_op jit(solution)/shard_map/ppermute | solution.py:301
  131.9 7.5 %collective-permute-start.22 = (bf16[16,8,384]{2,1,0:T(8,128)(2,1)S(1)}, bf16[16,8,384]{2,1,0:T(8,128)(2,1)S(1)}, u32[]{:S(2)}, u32[]{:S(2)}) collective-permute-start(bf16[16,8,384]{2,1,0:T(8,128)(2,1)S(1)} %all_to_all.11.refs_0_), channel_id=1, source_target_pairs={{0,1},{1,2},{2,3},{3,0},{4,5},{5,6},{6,7},{7,4},{8,9},{9,10},{10,1... | collective-permute-start | bytes 294920 | tf_op jit(solution)/shard_map/ppermute | solution.py:301
